TPU v7x, 256 devices: a whole 4x4x8 slice. The times are simulated.
256 devices in a mesh: section: 16 (over z_lo, y, core), dp: 16 (over z_hi, x).
Axes of the slice: x: 4, y: 4, z: 8 (z_hi: 4, z_lo: 2; z = z_hi * 2 + z_lo), core: 2. Of those that a mesh axis runs over, the one named last changes fastest.
Arguments:
- w_in: bfloat16 [16, 5120, 4096], P('section', 'dp'), may hold values from -0.09375 to 0.09375
- w_out: bfloat16 [16, 5120, 4096], P('section', 'dp'), may hold values from -0.078125 to 0.078125
- input_stash: bfloat16 [16, 2, 128, 4096], P('section', None, 'dp'), may hold values from -6 to 6
- hidden_stash: bfloat16 [16, 2, 128, 5120], P('section', None, None, 'dp'), may hold values from -6 to 6
- gate_stash: float32 [16, 2, 128], P('section'), may hold values from 0.25 to 1
- block_pick: int32 [16, 2], P('section'), may hold values from 0 to 1
- slot_order: int32 [16, 2], P('section'), may hold values from 0 to 1, each once within a row
- arriving: bfloat16 [16, 2, 128, 4096], P('section', None, 'dp'), may hold values from -6 to 6
- loss_grads: bfloat16 [1, 2, 128, 4096], P(None, None, 'dp'), may hold values from -6 to 6
Outputs:
- passed: bfloat16 [16, 2, 2, 128, 4096], P('section', None, None, 'dp')
- grad_in: bfloat16 [16, 5120, 4096], P('section', 'dp')
- grad_out: bfloat16 [16, 5120, 4096], P('section', 'dp')
- gate_grads: float32 [16, 2, 128], P('section')
Inputs may be any that keep to these rules, and one draw needn't show every extreme that they name: Each row of slot_order holds every slot 0 to 1 once.
All inputs are finite; a program needn't handle non-finite values.
Results may differ from a plain program's by a relative error of at most 0.0055.
Values may be sent and summed in bfloat16 or wider, within the bound.
A program may use at most 128 MiB of HBM per device.

v0:
```python
import jax
import jax.numpy as jnp
from jax import lax
from jax.sharding import PartitionSpec as P


def shifted_2(block, axis, distance):
    devices = range(lax.axis_size(axis))
    route = [(i - distance, i) for i in devices if i - distance in devices]
    return lax.ppermute(block, axis, route)


def per_device(
    w_in, w_out, input_stash, hidden_stash, gate_stash, block_pick, slot_order, arriving, loss_grads
):
    in_weight = w_in[0]
    out_weight = w_out[0]
    ticks = slot_order.shape[1]
    blocks = arriving.shape[1]
    is_top = lax.axis_index("section") == lax.axis_size("section") - 1
    contract = (((0,), (0,)), ((), ()))

    def section_tick(incoming, tick_index):
        slot_id = slot_order[0, tick_index]
        block_id = block_pick[0, slot_id]
        gate_vals = gate_stash[0, slot_id]
        pre_act = hidden_stash[0, slot_id]
        own_rows = incoming[block_id]
        rows_input, rows_grad = (
            lax.all_gather(input_stash[0, slot_id], "dp", axis=0, tiled=True),
            lax.all_gather(own_rows, "dp", axis=0, tiled=True),
        )
        upstream = lax.dot_general(
            rows_grad, out_weight, (((1,), (1,)), ((), ())), preferred_element_type=jnp.float32
        )
        active = jnp.maximum(pre_act.astype(jnp.float32), 0.0)
        hid_grad = jnp.where(pre_act > 0, upstream * gate_vals[:, None], 0.0).astype(jnp.bfloat16)
        input_part = lax.psum_scatter(
            jnp.dot(hid_grad, in_weight, preferred_element_type=jnp.float32),
            "dp",
            scatter_dimension=0,
            tiled=True,
        )
        placed = jnp.where((jnp.arange(blocks) == block_id)[:, None, None], input_part[None], 0.0)
        updated = (incoming.astype(jnp.float32) + placed).astype(jnp.bfloat16)
        gate_part = jnp.sum(active * upstream, axis=1)
        gate_part = lax.psum(gate_part, "dp")
        weighted = (active * gate_vals[:, None]).astype(jnp.bfloat16)
        return (updated, gate_part, (rows_grad, weighted, hid_grad, rows_input))

    def weight_terms(pieces):
        rows_grad, weighted, hid_grad, rows_input = pieces
        out_term = lax.dot_general(
            weighted, rows_grad, contract, preferred_element_type=jnp.float32
        )
        in_term = lax.dot_general(
            hid_grad, rows_input, contract, preferred_element_type=jnp.float32
        )
        return (out_term, in_term)

    start_sums = (jnp.zeros(out_weight.shape, jnp.float32), jnp.zeros(in_weight.shape, jnp.float32))

    def advance(carry, extra):
        incoming, sums = carry
        tick_index, loss_rows = extra
        updated, gate_part, pieces = section_tick(incoming, tick_index)
        terms = weight_terms(pieces)
        sums = (sums[0] + terms[0], sums[1] + terms[1])
        shifted = shifted_2(updated, "section", -1)
        following = jnp.where(is_top, loss_rows, shifted)
        return ((following, sums), (updated, gate_part))

    (last_in, sums), (early_out, early_gate) = lax.scan(
        advance, (arriving[0], start_sums), (jnp.arange(ticks - 1), loss_grads)
    )
    last_out, last_gate, last_pieces = section_tick(last_in, ticks - 1)
    terms = weight_terms(last_pieces)
    out_sum = sums[0] + terms[0]
    in_sum = sums[1] + terms[1]
    passed = jnp.concatenate([early_out, last_out[None]], axis=0)
    gate_parts = jnp.concatenate([early_gate, last_gate[None]], axis=0)
    onehot = (slot_order[0][:, None] == jnp.arange(ticks)[None, :]).astype(jnp.float32)
    gate_grads = jnp.einsum("tp,tr->pr", onehot, gate_parts, precision=lax.Precision.HIGHEST)
    return (
        passed[None],
        in_sum.astype(jnp.bfloat16)[None],
        out_sum.astype(jnp.bfloat16)[None],
        gate_grads[None],
    )


def solution(mesh):
    placed = (
        P("section", "dp", None),
        P("section", "dp", None),
        P("section", None, "dp", None),
        P("section", None, None, "dp"),
        P("section", None, None),
        P("section", None),
        P("section", None),
        P("section", None, "dp", None),
        P(None, None, "dp", None),
    )
    return jax.shard_map(
        per_device,
        mesh=mesh,
        in_specs=placed,
        out_specs=(
            P("section", None, None, "dp", None),
            P("section", "dp", None),
            P("section", "dp", None),
            P("section", None, None),
        ),
        check_vma=False,
    )
```

profile of v0, /device:TPU:8, one launch (start us, length us, event | category | flops | bytes accessed | tf_op | source)
XLA Modules:
  0.0 431.0 jit_solution(4442010572938618943)
XLA Ops:
  7.2 0.0 copy-start
  7.2 0.0 all-gather.9.cloned.1.call-start
  7.2 1.4 fusion.47
  12.5 1.3 constant_dynamic-slice_fusion.4
  15.8 1.5 constant_dynamic-slice_fusion.6
  17.3 0.0 all-gather.9.cloned.1.call-update
  17.3 0.0 reduce-scatter.3.cloned.1.call-start
  17.3 0.8 fusion.42
  18.1 56.0 %all-gather.9.cloned.1.call-done = bf16[1,1,128,4096]{3,2,1,0:T(8,128)(2,1)} async-done(((bf16[1,1,8,4096]{3,2,1,0:T(8,128)(2,1)}), bf16[1,1,128,4096]{3,2,1,0:T(8,128)(2,1)}) %all-gather.9.cloned.1.call-update) | async-done | bytes 1048592 | tf_op jit(solution)/shard_map/while/body/eval_jaxpr/all_gather | solution.py:31
  74.1 2.9 select_convert_fusion.1
  76.9 0.0 copy-done
  76.9 0.0 copy-start.2
  77.0 0.0 copy-start.4
  77.0 2.1 fusion.6
  79.0 0.0 copy-start.1
  79.0 0.0 reduce-scatter.3.cloned.1.call-update
  79.1 0.0 all-gather.11.cloned.1.call-start
  79.1 0.7 iota_compare_fusion.1
  79.8 85.0 %reduce-scatter.3.cloned.1.call-done = f32[8,4096]{1,0:T(8,128)} async-done(((f32[128,4096]{1,0:T(8,128)}), f32[8,4096]{1,0:T(8,128)}) %reduce-scatter.3.cloned.1.call-update) | async-done | bytes 131088 | tf_op jit(solution)/shard_map/while/body/eval_jaxpr/reduce_scatter | solution.py:38
  164.7 0.0 copy-done.2
  164.7 1.0 fusion.22
  165.7 1.9 collective-permute-start
  169.6 0.6 collective-permute-done
  170.2 0.0 copy-done.4
  170.2 0.9 bitcast_select_fusion
  171.1 0.6 constant_dynamic-slice_fusion.3
  171.7 0.0 all-gather.11.cloned.1.call-update
  171.8 0.0 all-gather.13.cloned.1.call-start
  171.8 1.5 constant_dynamic-slice_fusion
  173.4 0.0 all-gather.13.cloned.1.call-update
  173.4 0.0 all-gather.15.cloned.1.call-start
  173.4 0.5 all-gather.15.cloned.1.call-update
  174.0 0.0 reduce-scatter.5.cloned.1.call-start
  174.0 51.0 %all-gather.11.cloned.1.call-done = bf16[1,128,4096]{2,1,0:T(8,128)(2,1)} async-done(((bf16[1,8,4096]{2,1,0:T(8,128)(2,1)}), bf16[1,128,4096]{2,1,0:T(8,128)(2,1)}) %all-gather.11.cloned.1.call-update) | async-done | bytes 1048592 | tf_op jit(solution)/shard_map/all_gather | solution.py:31
  225.0 0.0 copy-done.1
  225.0 2.9 fusion.26
  227.9 2.1 fusion.4
  230.0 0.0 reduce-scatter.5.cloned.1.call-update
  230.0 0.7 iota_compare_fusion
  230.7 4.4 %fusion.17 = f32[320,4096]{1,0:T(8,128)} fusion(bf16[1,1,128,4096]{3,2,1,0:T(8,128)(2,1)} %all-gather.9.cloned.1.call-done, f32[128]{0:T(128)S(1)} %get-tuple-element.42, bf16[1,2,128,320]{2,3,1,0:T(8,128)(2,1)S(1)} %copy-done.1, s32[]{:T(128)S(6)} %select_n.57), kind=kOutput, calls=%fused_computation.20 | convolution fusion | flops 335708160 | bytes 6373892 | tf_op jit(solution)/shard_map/while/body/eval_jaxpr/dot_general | solution.py:53
  235.1 0.0 copy-start.3
  235.1 0.0 copy-start.5
  235.1 43.8 %all-gather.13.cloned.1.call-done = bf16[1,1,128,4096]{3,2,1,0:T(8,128)(2,1)} async-done(((bf16[1,1,8,4096]{3,2,1,0:T(8,128)(2,1)}), bf16[1,1,128,4096]{3,2,1,0:T(8,128)(2,1)}) %all-gather.13.cloned.1.call-update) | async-done | bytes 1048592 | tf_op jit(solution)/shard_map/while/body/eval_jaxpr/all_gather | solution.py:30
  278.9 4.4 %fusion.13 = f32[320,4096]{1,0:T(8,128)} fusion(bf16[128,320]{0,1:T(8,128)(2,1)S(1)} %get-tuple-element.62, bf16[1,1,128,4096]{3,2,1,0:T(8,128)(2,1)} %all-gather.13.cloned.1.call-done), kind=kOutput, calls=%fused_computation.16 | convolution fusion | flops 335544320 | bytes 6373376 | tf_op jit(solution)/shard_map/while/body/eval_jaxpr/dot_general | solution.py:56
  283.3 0.0 copy-done.3
  283.3 0.1 fusion.20
  283.4 42.8 %all-reduce = (f32[1,128]{1,0:T(1,128)S(1)}, f32[1,128]{1,0:T(1,128)S(1)}) all-reduce(f32[1,128]{1,0:T(1,128)S(1)} %bitcast.89, f32[1,128]{1,0:T(1,128)S(1)} %bitcast.88), channel_id=1, replica_groups=mesh['section'=16,'dp'=16] {'dp'}, use_global_device_ids=true, to_apply=%region_5.6 | all-reduce | flops 256 | bytes 2048 | tf_op jit(solution)/shard_map/psum | solution.py:47
  326.2 0.0 copy-done.5
  326.2 0.8 convolution_bitcast_fusion
  327.0 5.2 %fusion.2 = bf16[1,320,4096]{2,1,0:T(8,128)(2,1)} fusion(f32[320,4096]{1,0:T(8,128)} %fusion.17, bf16[1,128,4096]{2,1,0:T(8,128)(2,1)} %all-gather.11.cloned.1.call-done, f32[128]{0:T(128)S(1)} %get-tuple-element.41, bf16[1,2,128,320]{2,3,1,0:T(8,128)(2,1)S(1)} %copy-done.1, s32[]{:T(128)S(6)} %select_n.64), kind=kOutput, calls=%fused_computation.4 | convolution fusion | flops 338329600 | bytes 8995332 | tf_op jit(solution)/shard_map/dot_general | solution.py:53
  332.1 0.2 all-gather.15.cloned.1.call-done
  332.3 5.1 %fusion.3 = bf16[1,320,4096]{2,1,0:T(8,128)(2,1)} fusion(f32[320,4096]{1,0:T(8,128)} %fusion.13, bf16[128,320]{0,1:T(8,128)(2,1)S(1)} %get-tuple-element.38, bf16[1,1,128,4096]{3,2,1,0:T(8,128)(2,1)} %all-gather.15.cloned.1.call-done), kind=kOutput, calls=%fused_computation.5 | convolution fusion | flops 338165760 | bytes 8994816 | tf_op jit(solution)/shard_map/dot_general | solution.py:56
  337.4 84.9 %reduce-scatter.5.cloned.1.call-done = f32[8,4096]{1,0:T(8,128)} async-done(((f32[128,4096]{1,0:T(8,128)}), f32[8,4096]{1,0:T(8,128)}) %reduce-scatter.5.cloned.1.call-update) | async-done | bytes 131088 | tf_op jit(solution)/shard_map/reduce_scatter | solution.py:38
  422.4 1.0 fusion.27
  423.4 0.7 maximum_bitcast_fusion
Async XLA Ops:
  7.2 69.8 %copy-start = (bf16[1,320,4096]{2,1,0:T(8,128)(2,1)S(1)}, bf16[1,320,4096]{2,1,0:T(8,128)(2,1)}, u32[]{:S(2)}) copy-start(bf16[1,320,4096]{2,1,0:T(8,128)(2,1)} %param.9) | copy-start | bytes 7864324
  7.2 66.9 %all-gather.9.cloned.1.call-start = ((), (), s32[]{:S(2)}) async-start(), calls=%async_computation.4 | async-start | bytes 1114112 | tf_op jit(solution)/shard_map/while/body/eval_jaxpr/all_gather | solution.py:31
  17.3 147.5 %reduce-scatter.3.cloned.1.call-start = ((), (), s32[]{:S(2)}) async-start(), calls=%async_computation.2 | async-start | bytes 2228224 | tf_op jit(solution)/shard_map/while/body/eval_jaxpr/reduce_scatter | solution.py:38
  76.9 87.8 %copy-start.2 = (bf16[1,2,8,4096]{3,2,1,0:T(8,128)(2,1)S(1)}, bf16[1,2,8,4096]{3,2,1,0:T(8,128)(2,1)}, u32[]{:S(2)}) copy-start(bf16[1,2,8,4096]{3,2,1,0:T(8,128)(2,1)} %param.16) | copy-start | bytes 393220
  77.0 93.2 %copy-start.4 = (bf16[1,2,8,4096]{3,2,1,0:T(8,128)(2,1)S(1)}, bf16[1,2,8,4096]{3,2,1,0:T(8,128)(2,1)}, u32[]{:S(2)}) copy-start(bf16[1,2,8,4096]{3,2,1,0:T(8,128)(2,1)} %param.17) | copy-start | bytes 393220
  79.0 145.9 %copy-start.1 = (bf16[1,2,128,320]{2,3,1,0:T(8,128)(2,1)S(1)}, bf16[1,2,128,320]{2,3,1,0:T(8,128)(2,1)}, u32[]{:S(2)}) copy-start(bf16[1,2,128,320]{2,3,1,0:T(8,128)(2,1)} %param.12) | copy-start | bytes 491524
  79.1 145.9 %all-gather.11.cloned.1.call-start = ((), (), s32[]{:S(2)}) async-start(), calls=%async_computation.5 | async-start | bytes 1114112 | tf_op jit(solution)/shard_map/all_gather | solution.py:31
  165.7 4.4 %collective-permute-start = (bf16[2,8,4096]{2,1,0:T(8,128)(2,1)S(1)}, bf16[2,8,4096]{2,1,0:T(8,128)(2,1)}, u32[]{:S(2)}, u32[]{:S(2)}) collective-permute-start(bf16[2,8,4096]{2,1,0:T(8,128)(2,1)S(1)} %fusion.22), channel_id=1, source_target_pairs={{16,0},{32,16},{48,32},{64,48},{80,64},{96,80},{112,96},{128,112},... | collective-permute-start | bytes 393224 | tf_op jit(solution)/shard_map/while/body/eval_jaxpr/ppermute | solution.py:10
  171.8 107.1 %all-gather.13.cloned.1.call-start = ((), (), s32[]{:S(2)}) async-start(), calls=%async_computation.6 | async-start | bytes 1114112 | tf_op jit(solution)/shard_map/while/body/eval_jaxpr/all_gather | solution.py:30
  173.4 158.9 %all-gather.15.cloned.1.call-start = ((), (), s32[]{:S(2)}) async-start(), calls=%async_computation.7 | async-start | bytes 1114112 | tf_op jit(solution)/shard_map/all_gather | solution.py:30
  174.0 248.4 %reduce-scatter.5.cloned.1.call-start = ((), (), s32[]{:S(2)}) async-start(), calls=%async_computation.3 | async-start | bytes 2228224 | tf_op jit(solution)/shard_map/reduce_scatter | solution.py:38
  235.1 48.2 %copy-start.3 = (f32[8,4096]{1,0:T(8,128)S(1)}, f32[8,4096]{1,0:T(8,128)}, u32[]{:S(2)}) copy-start(f32[8,4096]{1,0:T(8,128)} %reduce-scatter.3.cloned.1.call-done) | copy-start | bytes 393220
  235.1 91.1 %copy-start.5 = (s32[1,2]{1,0:T(1,128)S(1)}, s32[1,2]{1,0:T(1,128)}, u32[]{:S(2)}) copy-start(s32[1,2]{1,0:T(1,128)} %param.15) | copy-start | bytes 28
Sparse Core Ops, SparseCore 0:
  17.4 56.6 all-gather.8
  79.2 85.5 reduce-scatter.2
  171.9 53.0 all-gather.10
  228.1 50.7 all-gather.12
  282.1 50.1 all-gather.14
  336.1 86.1 reduce-scatter.4
where the time goes:
time: 432 us; the launch traced here: 431 us
  waiting for transfers between devices  322 us (75%)
  blocking collectives  42.8 us (10%)
  matrix products  29.8 us (7%)
  between operations  22 us (5%)
  local copies, waits for them, and re-layouts  7.18 us (2%)
  other arithmetic  5.06 us (1%)
    reduce_scatter x2, waiting for transfers between devices, section_tick(): lax.psum_scatter(jnp.dot(hid_grad, in_weight, preferred_element_type=jnp....  170 us
    all_gather x2, waiting for transfers between devices, section_tick(): lax.all_gather(own_rows, 'dp', axis=0, tiled=True)  107 us
    all_gather x2, waiting for transfers between devices, section_tick(): lax.all_gather(input_stash[0, slot_id], 'dp', axis=0, tiled=True)  44 us
    psum x1, blocking collectives, section_tick(): gate_part = lax.psum(gate_part, 'dp')  42.8 us
    dot_general x2, matrix products, weight_terms(): lax.dot_general(weighted, rows_grad, contract, preferred_element_type=jnp...  9.57 us
    dot_general x2, matrix products, weight_terms(): lax.dot_general(hid_grad, rows_input, contract, preferred_element_type=jn...  9.5 us
  transfers between devices with their start and end apart: 7, of which 7 were waited for; matrix products, arithmetic and copies ran while one was open for 7% of the time, Pallas kernels for 0%

commit v1 on v0

--- a/solution.py
+++ b/solution.py
@@ -27,7 +27,12 @@
         pre_act = hidden_stash[0, slot_id]
         own_rows = incoming[block_id]
         rows_input, rows_grad = (
-            lax.all_gather(input_stash[0, slot_id], "dp", axis=0, tiled=True),
+            jnp.concatenate(
+                lax.all_to_all(
+                    jnp.stack([input_stash[0, slot_id]] * lax.axis_size("dp")), "dp", 0, 0
+                ),
+                axis=0,
+            ),
             lax.all_gather(own_rows, "dp", axis=0, tiled=True),
         )
         upstream = lax.dot_general(

time: 432 us -> 355 us (0.82)
  waiting for transfers between devices: 322 us -> 222 us
  blocking collectives: 42.8 us -> 54.6 us
  starting transfers between devices: 2.17 us -> 12.6 us
    reduce_scatter x2, waiting for transfers between devices: 170 us -> 106 us  [section_tick(): lax.psum_scatter(jnp.dot(hid_grad, in_weight, preferred_element_type=jnp....]
    all_gather x2 -> x0, waiting for transfers between devices: 44 us -> none  [section_tick(): lax.all_gather(input_stash[0, slot_id], 'dp', axis=0, tiled=True)]
    psum x1, blocking collectives: 42.8 us -> 54.6 us  [section_tick(): gate_part = lax.psum(gate_part, 'dp')]
    all_to_all x0 -> x2, starting transfers between devices: none -> 10.5 us  [section_tick(): lax.all_to_all(jnp.stack([input_stash[0, slot_id]] * lax.axis_size('dp'))...]
    all_gather x2, waiting for transfers between devices: 107 us -> 115 us  [section_tick(): lax.all_gather(own_rows, 'dp', axis=0, tiled=True)]
  transfers between devices with their start and end apart: 7 -> 7, of which waited for: 7 -> 5; matrix products, arithmetic and copies ran while one was open for 7% -> 9% of each run, Pallas kernels for 0% -> 0%
where the time goes in v1:
time: 355 us; the launch traced here: 354 us
  waiting for transfers between devices  222 us (63%)
  blocking collectives  54.6 us (15%)
  matrix products  29.9 us (8%)
  between operations  21.7 us (6%)
  starting transfers between devices  12.6 us (4%)
  local copies, waits for them, and re-layouts  8.68 us (2%)
  other arithmetic  5.09 us (1%)
    all_gather x2, waiting for transfers between devices, section_tick(): lax.all_gather(own_rows, 'dp', axis=0, tiled=True)  115 us
    reduce_scatter x2, waiting for transfers between devices, section_tick(): lax.psum_scatter(jnp.dot(hid_grad, in_weight, preferred_element_type=jnp....  106 us
    psum x1, blocking collectives, section_tick(): gate_part = lax.psum(gate_part, 'dp')  54.6 us
    all_to_all x2, starting transfers between devices, section_tick(): lax.all_to_all(jnp.stack([input_stash[0, slot_id]] * lax.axis_size('dp'))...  10.5 us
    dot_general x2, matrix products, weight_terms(): lax.dot_general(weighted, rows_grad, contract, preferred_element_type=jnp...  9.58 us
    dot_general x2, matrix products, weight_terms(): lax.dot_general(hid_grad, rows_input, contract, preferred_element_type=jn...  9.54 us
  transfers between devices with their start and end apart: 7, of which 5 were waited for; matrix products, arithmetic and copies ran while one was open for 9% of the time, Pallas kernels for 0%

profile of v1, /device:TPU:8, one launch (start us, length us, event | category | flops | bytes accessed | tf_op | source)
XLA Modules:
  0.0 354.2 jit_solution(11251658214536828007)
XLA Ops:
  7.2 0.0 copy-start
  7.2 0.0 all-gather.5.cloned.1.call-start
  7.2 1.4 fusion.47
  12.5 1.3 constant_dynamic-slice_fusion.2
  15.8 1.5 constant_dynamic-slice_fusion.4
  17.3 0.0 all-gather.5.cloned.1.call-update
  17.3 0.0 reduce-scatter.3.cloned.1.call-start
  17.3 0.8 fusion.42
  18.1 56.0 %all-gather.5.cloned.1.call-done = bf16[1,1,128,4096]{3,2,1,0:T(8,128)(2,1)} async-done(((bf16[1,1,8,4096]{3,2,1,0:T(8,128)(2,1)}), bf16[1,1,128,4096]{3,2,1,0:T(8,128)(2,1)}) %all-gather.5.cloned.1.call-update) | async-done | bytes 1048592 | tf_op jit(solution)/shard_map/while/body/eval_jaxpr/all_gather | solution.py:36
  74.1 2.9 select_convert_fusion.1
  76.9 0.0 copy-done
  76.9 0.0 copy-start.2
  77.0 0.0 copy-start.4
  77.0 2.1 fusion.6
  79.0 0.0 reduce-scatter.3.cloned.1.call-update
  79.1 0.0 copy-start.1
  79.1 0.0 all-gather.7.cloned.1.call-start
  79.1 0.7 iota_compare_fusion.1
  79.8 84.9 %reduce-scatter.3.cloned.1.call-done = f32[8,4096]{1,0:T(8,128)} async-done(((f32[128,4096]{1,0:T(8,128)}), f32[8,4096]{1,0:T(8,128)}) %reduce-scatter.3.cloned.1.call-update) | async-done | bytes 131088 | tf_op jit(solution)/shard_map/while/body/eval_jaxpr/reduce_scatter | solution.py:43
  164.7 0.0 copy-done.2
  164.7 1.0 fusion.22
  165.7 1.9 collective-permute-start
  169.6 0.6 collective-permute-done
  170.2 0.0 copy-done.4
  170.2 0.9 bitcast_select_fusion
  171.1 0.6 constant_dynamic-slice_fusion.1
  171.7 0.0 all-gather.7.cloned.1.call-update
  171.8 0.9 dynamic-slice_bitcast_fusion
  172.7 1.1 stack.7
  173.7 5.4 %all-to-all-start = ((bf16[16,8,4096]{2,1,0:T(8,128)(2,1)}), bf16[16,8,4096]{2,1,0:T(8,128)(2,1)}, u32[]{:S(2)}, u32[]{:S(2)}) async-start(bf16[16,8,4096]{2,1,0:T(8,128)(2,1)} %stack.7), calls=%async_computation.2 | async-start | bytes 2097152 | tf_op jit(solution)/shard_map/while/body/eval_jaxpr/all_to_all | solution.py:31
  179.2 0.0 reduce-scatter.5.cloned.1.call-start
  179.2 58.8 %all-gather.7.cloned.1.call-done = bf16[1,128,4096]{2,1,0:T(8,128)(2,1)} async-done(((bf16[1,8,4096]{2,1,0:T(8,128)(2,1)}), bf16[1,128,4096]{2,1,0:T(8,128)(2,1)}) %all-gather.7.cloned.1.call-update) | async-done | bytes 1048592 | tf_op jit(solution)/shard_map/all_gather | solution.py:36
  238.0 0.0 copy-done.1
  238.0 2.9 fusion.26
  240.9 2.1 fusion.4
  243.0 0.0 reduce-scatter.5.cloned.1.call-update
  243.0 0.7 iota_compare_fusion
  243.7 0.0 all-to-all-done
  243.7 1.1 stack.8
  244.8 5.1 %all-to-all-start.1 = ((bf16[16,8,4096]{2,1,0:T(8,128)(2,1)}), bf16[16,8,4096]{2,1,0:T(8,128)(2,1)}, u32[]{:S(2)}, u32[]{:S(2)}) async-start(bf16[16,8,4096]{2,1,0:T(8,128)(2,1)} %stack.8), calls=%async_computation.3 | async-start | bytes 2097152 | tf_op jit(solution)/shard_map/all_to_all | solution.py:31
  249.9 4.4 %fusion.17 = f32[320,4096]{1,0:T(8,128)} fusion(bf16[1,1,128,4096]{3,2,1,0:T(8,128)(2,1)} %all-gather.5.cloned.1.call-done, f32[128]{0:T(128)S(1)} %get-tuple-element.42, bf16[1,2,128,320]{2,3,1,0:T(8,128)(2,1)S(1)} %copy-done.1, s32[]{:T(128)S(6)} %select_n.57), kind=kOutput, calls=%fused_computation.20 | convolution fusion | flops 335708160 | bytes 6373892 | tf_op jit(solution)/shard_map/while/body/eval_jaxpr/dot_general | solution.py:58
  254.3 0.0 copy-start.3
  254.3 0.0 copy-start.5
  254.3 4.4 %fusion.13 = f32[320,4096]{1,0:T(8,128)} fusion(bf16[128,320]{0,1:T(8,128)(2,1)S(1)} %get-tuple-element.62, bf16[16,8,4096]{2,1,0:T(8,128)(2,1)} %all-to-all-done), kind=kOutput, calls=%fused_computation.16 | convolution fusion | flops 335544320 | bytes 6373376 | tf_op jit(solution)/shard_map/while/body/eval_jaxpr/dot_general | solution.py:61
  258.7 0.0 copy-done.3
  258.7 0.1 fusion.20
  258.8 54.6 %all-reduce = (f32[1,128]{1,0:T(1,128)S(1)}, f32[1,128]{1,0:T(1,128)S(1)}) all-reduce(f32[1,128]{1,0:T(1,128)S(1)} %bitcast.93, f32[1,128]{1,0:T(1,128)S(1)} %bitcast.92), channel_id=1, replica_groups=mesh['section'=16,'dp'=16] {'dp'}, use_global_device_ids=true, to_apply=%region_5.6 | all-reduce | flops 256 | bytes 2048 | tf_op jit(solution)/shard_map/psum | solution.py:52
  313.4 0.0 copy-done.5
  313.4 0.8 convolution_bitcast_fusion
  314.2 5.2 %fusion.2 = bf16[1,320,4096]{2,1,0:T(8,128)(2,1)} fusion(f32[320,4096]{1,0:T(8,128)} %fusion.17, bf16[1,128,4096]{2,1,0:T(8,128)(2,1)} %all-gather.7.cloned.1.call-done, f32[128]{0:T(128)S(1)} %get-tuple-element.41, bf16[1,2,128,320]{2,3,1,0:T(8,128)(2,1)S(1)} %copy-done.1, s32[]{:T(128)S(6)} %select_n.64), kind=kOutput, calls=%fused_computation.4 | convolution fusion | flops 338329600 | bytes 8995332 | tf_op jit(solution)/shard_map/dot_general | solution.py:58
  319.4 0.0 all-to-all-done.1
  319.4 5.1 %fusion.3 = bf16[1,320,4096]{2,1,0:T(8,128)(2,1)} fusion(f32[320,4096]{1,0:T(8,128)} %fusion.13, bf16[128,320]{0,1:T(8,128)(2,1)S(1)} %get-tuple-element.38, bf16[16,8,4096]{2,1,0:T(8,128)(2,1)} %all-to-all-done.1), kind=kOutput, calls=%fused_computation.5 | convolution fusion | flops 338165760 | bytes 8994816 | tf_op jit(solution)/shard_map/dot_general | solution.py:61
  324.6 21.3 %reduce-scatter.5.cloned.1.call-done = f32[8,4096]{1,0:T(8,128)} async-done(((f32[128,4096]{1,0:T(8,128)}), f32[8,4096]{1,0:T(8,128)}) %reduce-scatter.5.cloned.1.call-update) | async-done | bytes 131088 | tf_op jit(solution)/shard_map/reduce_scatter | solution.py:43
  345.9 1.0 fusion.27
  346.9 0.7 maximum_bitcast_fusion
Async XLA Ops:
  7.2 69.8 %copy-start = (bf16[1,320,4096]{2,1,0:T(8,128)(2,1)S(1)}, bf16[1,320,4096]{2,1,0:T(8,128)(2,1)}, u32[]{:S(2)}) copy-start(bf16[1,320,4096]{2,1,0:T(8,128)(2,1)} %param.9) | copy-start | bytes 7864324
  7.2 66.9 %all-gather.5.cloned.1.call-start = ((), (), s32[]{:S(2)}) async-start(), calls=%async_computation.6 | async-start | bytes 1114112 | tf_op jit(solution)/shard_map/while/body/eval_jaxpr/all_gather | solution.py:36
  17.3 147.5 %reduce-scatter.3.cloned.1.call-start = ((), (), s32[]{:S(2)}) async-start(), calls=%async_computation.4 | async-start | bytes 2228224 | tf_op jit(solution)/shard_map/while/body/eval_jaxpr/reduce_scatter | solution.py:43
  76.9 87.8 %copy-start.2 = (bf16[1,2,8,4096]{3,2,1,0:T(8,128)(2,1)S(1)}, bf16[1,2,8,4096]{3,2,1,0:T(8,128)(2,1)}, u32[]{:S(2)}) copy-start(bf16[1,2,8,4096]{3,2,1,0:T(8,128)(2,1)} %param.16) | copy-start | bytes 393220
  77.0 93.2 %copy-start.4 = (bf16[1,2,8,4096]{3,2,1,0:T(8,128)(2,1)S(1)}, bf16[1,2,8,4096]{3,2,1,0:T(8,128)(2,1)}, u32[]{:S(2)}) copy-start(bf16[1,2,8,4096]{3,2,1,0:T(8,128)(2,1)} %param.17) | copy-start | bytes 393220
  79.1 158.9 %copy-start.1 = (bf16[1,2,128,320]{2,3,1,0:T(8,128)(2,1)S(1)}, bf16[1,2,128,320]{2,3,1,0:T(8,128)(2,1)}, u32[]{:S(2)}) copy-start(bf16[1,2,128,320]{2,3,1,0:T(8,128)(2,1)} %param.12) | copy-start | bytes 491524
  79.1 158.9 %all-gather.7.cloned.1.call-start = ((), (), s32[]{:S(2)}) async-start(), calls=%async_computation.7 | async-start | bytes 1114112 | tf_op jit(solution)/shard_map/all_gather | solution.py:36
  165.7 4.4 %collective-permute-start = (bf16[2,8,4096]{2,1,0:T(8,128)(2,1)S(1)}, bf16[2,8,4096]{2,1,0:T(8,128)(2,1)}, u32[]{:S(2)}, u32[]{:S(2)}) collective-permute-start(bf16[2,8,4096]{2,1,0:T(8,128)(2,1)S(1)} %fusion.22), channel_id=1, source_target_pairs={{16,0},{32,16},{48,32},{64,48},{80,64},{96,80},{112,96},{128,112},... | collective-permute-start | bytes 393224 | tf_op jit(solution)/shard_map/while/body/eval_jaxpr/ppermute | solution.py:10
  173.7 69.9 %all-to-all-start = ((bf16[16,8,4096]{2,1,0:T(8,128)(2,1)}), bf16[16,8,4096]{2,1,0:T(8,128)(2,1)}, u32[]{:S(2)}, u32[]{:S(2)}) async-start(bf16[16,8,4096]{2,1,0:T(8,128)(2,1)} %stack.7), calls=%async_computation.2 | async-start | bytes 2097152 | tf_op jit(solution)/shard_map/while/body/eval_jaxpr/all_to_all | solution.py:31
  179.2 166.7 %reduce-scatter.5.cloned.1.call-start = ((), (), s32[]{:S(2)}) async-start(), calls=%async_computation.5 | async-start | bytes 2228224 | tf_op jit(solution)/shard_map/reduce_scatter | solution.py:43
  244.8 74.7 %all-to-all-start.1 = ((bf16[16,8,4096]{2,1,0:T(8,128)(2,1)}), bf16[16,8,4096]{2,1,0:T(8,128)(2,1)}, u32[]{:S(2)}, u32[]{:S(2)}) async-start(bf16[16,8,4096]{2,1,0:T(8,128)(2,1)} %stack.8), calls=%async_computation.3 | async-start | bytes 2097152 | tf_op jit(solution)/shard_map/all_to_all | solution.py:31
  254.3 4.4 %copy-start.3 = (f32[8,4096]{1,0:T(8,128)S(1)}, f32[8,4096]{1,0:T(8,128)}, u32[]{:S(2)}) copy-start(f32[8,4096]{1,0:T(8,128)} %reduce-scatter.3.cloned.1.call-done) | copy-start | bytes 393220
  254.3 59.1 %copy-start.5 = (s32[1,2]{1,0:T(1,128)S(1)}, s32[1,2]{1,0:T(1,128)}, u32[]{:S(2)}) copy-start(s32[1,2]{1,0:T(1,128)} %param.15) | copy-start | bytes 28
Sparse Core Ops, SparseCore 0:
  17.4 56.6 all-gather.4
  79.2 85.5 reduce-scatter.2
  171.9 66.0 all-gather.6
  243.1 102.7 reduce-scatter.4
